TPU v7x, 32 devices: a whole 2x2x4 slice. The times are simulated.
32 devices in a mesh: snp: 8 (over z, y), samp: 4 (over x, core).
Axes of the slice: x: 2, y: 2, z: 4, core: 2. Of those that a mesh axis runs over, the one named last changes fastest.
Arguments:
- dosage: bfloat16 [5120, 8192], P('samp', 'snp'), may hold values from 0 to 2, as said below
- observed: int32 [5120, 8192], P('samp', 'snp'), may hold values 0 or 1
- band: int32 [8], replicated, may hold values from 1 to 2
Outputs:
- linkage: float32 [8192, 5120], P(('snp', 'samp'))
Inputs may be any that keep to these rules, and one draw needn't show every extreme that they name: `dosage`: real-valued dosages.
All inputs are finite; a program needn't handle non-finite values. No bound on the sum of `observed` on one device may be relied on, other than what follows from the above.
Results may differ from a plain program's by a relative error of at most 0.00055.
Values may be sent and summed in bfloat16 or wider, within the bound.
A program may use at most 128 MiB of HBM per device.

v0:
```python
import functools

import jax
import jax.numpy as jnp
from jax import lax
from jax.experimental import pallas as pl
from jax.experimental.pallas import tpu as pltpu
from jax.sharding import PartitionSpec as P

eps = 1e-05
MESH = pl.DeviceIdType.MESH
CHUNK = 256
TOP = 32767.0
RANGE = 2.0
CODE = TOP / RANGE**0.5


def offset_of(slot, e):
    return jnp.where(slot == 1, -e, jnp.where(slot == 2, -2 * e, jnp.where(slot == 3, 2 * e, jnp.where(slot == 4, e, 0))))


def encode(values):
    root = values * lax.rsqrt(jnp.maximum(jnp.abs(values), 1e-30)) * CODE
    code = jnp.round(jnp.clip(root, -TOP, TOP)).astype(jnp.int32)
    half = values.shape[0] // 2
    return lax.shift_left(code[:half], 16) | (code[half:] & 65535)


def decode(word):
    def value(code):
        f = code.astype(jnp.float32)
        return f * jnp.abs(f) * (1.0 / (CODE * CODE))

    return value(lax.shift_right_arithmetic(word, 16)), value(lax.shift_right_arithmetic(lax.shift_left(word, 16), 16))


def linkage_kernel(
    nblk, nsamp, nk, band_ref, dosage_ref, observed_ref, out_ref,
    dosages, marks, stats, zt, diag, part_out, part_in, diag_part_out, diag_part_in, diag_out, diag_in,
    dosage_sem, mark_sem, stat_send, stat_recv, z_send, z_recv, fwd_send, fwd_recv,
    part_send, part_recv, dpart_send, dpart_recv, diag_send, diag_recv,
):
    b = lax.axis_index("snp")
    s = lax.axis_index("samp")
    ngrp = nsamp // 2
    c = s % 2
    g = s // 2
    mate = s + 1 - 2 * c
    e = 2 * (b % 2) - 1
    width = nk * CHUNK
    rows = width // nsamp
    half = rows // 2

    def inside(block):
        return (block >= 0) & (block < nblk)

    def has(slot):
        return inside(b + offset_of(slot, e))

    npiece = nk + 1
    short = CHUNK // 2

    def columns(k):
        return pl.ds(pl.multiple_of(k * CHUNK, CHUNK), CHUNK)

    def chunk_at(slot, p):
        return jnp.where((slot < 2) | (p == 0), p, jnp.where(p == nk - 1, 1, p + 1))

    def place_of(slot, k):
        p = jnp.where((slot < 2) | (k == 0), k, jnp.where(k == 1, nk - 1, k - 1))
        return jnp.where(p == nk - 1, nk, p)

    def start_of(slot, p):
        return jnp.where(p < nk, chunk_at(slot, p) * CHUNK, chunk_at(slot, nk - 1) * CHUNK + short)

    def piece(slot, p, size):
        return pl.ds(pl.multiple_of(start_of(slot, p), short), size)

    def room(slot, start, size):
        return pl.ds(pl.multiple_of((offset_of(slot, e) + 2) * width + start, short), size)

    def load(k):
        part = pl.ds(k * CHUNK, CHUNK)
        return (
            pltpu.make_async_copy(dosage_ref.at[:, part], dosages.at[k], dosage_sem.at[k]),
            pltpu.make_async_copy(observed_ref.at[:, part], marks.at[k], mark_sem.at[k]),
        )

    for k in range(nk):
        for copy in load(k):
            copy.start()

    barrier = pltpu.get_barrier_semaphore()
    for j in range(1, nsamp):
        pl.semaphore_signal(barrier, inc=1, device_id=(b, (s + j) % nsamp), device_id_type=MESH)
    for slot in (1, 2, 3):
        @pl.when(has(slot))
        def _():
            pl.semaphore_signal(barrier, inc=1, device_id=(b + offset_of(slot, e), s), device_id_type=MESH)

    depth = dosages.shape[1]
    lanes = 128

    def tell(j, k):
        return pltpu.make_async_remote_copy(
            stats.at[s, k], stats.at[s, k], stat_send.at[j - 1, k], stat_recv.at[j - 1, k],
            device_id=(b, (s + j) % nsamp), device_id_type=MESH)

    def hear(j, k):
        other = (s + nsamp - j) % nsamp
        return pltpu.make_async_remote_copy(
            stats.at[other, k], stats.at[other, k], stat_send.at[j - 1, k], stat_recv.at[j - 1, k],
            device_id=(b, other), device_id_type=MESH)

    for k in range(nk):
        for copy in load(k):
            copy.wait()

        def add_rows(r, sums):
            at = pl.ds(pl.multiple_of(r * lanes, lanes), lanes)
            weight = marks[k, at, :].astype(jnp.float32)
            first = weight * dosages[k, at, :].astype(jnp.float32)
            second = first * dosages[k, at, :].astype(jnp.float32)
            return tuple(
                total + jnp.sum(term.reshape(lanes // 8, 8, CHUNK), axis=0)
                for total, term in zip(sums, (weight, first, second))
            )

        zero = jnp.zeros((8, CHUNK), jnp.float32)
        sums = lax.fori_loop(0, depth // lanes, add_rows, (zero, zero, zero))
        for q in range(3):
            stats[s, k, q : q + 1, :] = jnp.sum(sums[q], axis=0, keepdims=True)
        stats[s, k, 3:8, :] = jnp.zeros((5, CHUNK), jnp.float32)
        if k == 0:
            beside = [jnp.where(has(slot), 1, 0) for slot in (1, 2, 3)]
            pl.semaphore_wait(barrier, nsamp - 1 + sum(beside))
        for j in range(1, nsamp):
            tell(j, k).start()

    def direct(way, p, size):
        target = b + (-e, 2 * e, -2 * e)[way - 1]
        return target, pltpu.make_async_remote_copy(
            zt.at[0, c, piece(way, p, size)], zt.at[way, c, piece(way, p, size)], z_send.at[way, p], z_recv.at[way, p],
            device_id=(target, s), device_id_type=MESH)

    def arrival(slot, p, size):
        return pltpu.make_async_remote_copy(
            zt.at[slot, c, piece(slot, p, size)], zt.at[slot, c, piece(slot, p, size)], z_send.at[slot, p], z_recv.at[slot, p],
            device_id=(b, mate), device_id_type=MESH)

    def forward(slot, p, size):
        return pltpu.make_async_remote_copy(
            zt.at[slot, c, piece(slot, p, size)], zt.at[slot, c, piece(slot, p, size)], fwd_send.at[slot, p], fwd_recv.at[slot, p],
            device_id=(b, mate), device_id_type=MESH)

    def forward_in(slot, p, size):
        return pltpu.make_async_remote_copy(
            zt.at[slot, 1 - c, piece(slot, p, size)], zt.at[slot, 1 - c, piece(slot, p, size)],
            fwd_send.at[slot, p], fwd_recv.at[slot, p],
            device_id=(b, mate), device_id_type=MESH)

    sizes = [CHUNK] * (nk - 1) + [short, short]
    order = [0, *range(2, nk), 1]

    def send(way, p):
        target, copy = direct(way, p, sizes[p])

        @pl.when(inside(target))
        def _():
            copy.start()

    for k in range(nk):
        for j in range(1, nsamp):
            hear(j, k).wait_recv()
        part = stats[0, k]
        for other in range(1, nsamp):
            part = part + stats[other, k]
        cnt, first, second = part[0:1], part[1:2], part[2:3]
        mean = first / cnt
        scale = lax.rsqrt(second - first * mean + eps * cnt)

        def standardize(r, carry):
            at = pl.ds(pl.multiple_of(r * lanes, lanes), lanes)
            weight = marks[k, at, :].astype(jnp.float32)
            values = dosages[k, at, :].astype(jnp.float32)
            zed = (weight * (values - mean) * scale).astype(jnp.bfloat16)
            zt[0, c, columns(k), at] = zed.T
            return carry

        lax.fori_loop(0, depth // lanes, standardize, 0)
        for way in (1, 2, 3):
            done = range(k + 1)
            before = range(k)
            sequence = range(nk) if way == 1 else order
            def gone(chunks):
                n = 0
                while n < nk and sequence[n] in chunks:
                    n += 1
                return n
            for p in range(gone(before), gone(done)):
                send(way, p)
                if p == nk - 1:
                    send(way, nk)
        forward(0, k, CHUNK).start()

    def product(left, group, right, at):
        own_rows = pl.ds(pl.multiple_of((2 * group + c) * rows, rows), rows)
        both = [
            lax.dot_general(
                zt[left, h, own_rows, :], zt[right, h, at, :], (((1,), (1,)), ((), ())),
                preferred_element_type=jnp.float32)
            for h in range(2)
        ]
        return both[0] + both[1]

    def partial(i, j, size):
        return pltpu.make_async_remote_copy(
            part_out.at[i, j - 1, :, 0:size], part_in.at[i, j - 1, :, 0:size], part_send.at[i, j - 1], part_recv.at[i, j - 1],
            device_id=(b, 2 * ((g + j) % ngrp) + c), device_id_type=MESH)

    def multiply(slot, p, size, start):
        i = slot * npiece + p
        at = pl.ds(pl.multiple_of(start, short), size)
        for j in range(1, ngrp):
            part_out[i, j - 1, :, 0:size] = encode(product(0, (g + j) % ngrp, slot, at))
            partial(i, j, size).start()
        out_ref[:, room(slot, start, size)] = product(0, g, slot, at)

    def kept(slot):
        offset = offset_of(slot, e)
        inner = jnp.abs(offset) <= jnp.minimum(band_ref[b], band_ref[b + offset])
        return jnp.where(inner, 1.0, 0.0).astype(jnp.float32)

    def finish(slot, p, size, start):
        i = slot * npiece + p
        to = room(slot, start, size)
        upper, lower = out_ref[:half, to], out_ref[half:, to]
        for j in range(1, ngrp):
            partial(i, j, size).wait_recv()
            high, low = decode(part_in[i, j - 1, :, 0:size])
            upper, lower = upper + high, lower + low
        keep = kept(slot)
        out_ref[:half, to] = upper * keep
        out_ref[half:, to] = lower * keep

    makes = has(1) & has(2)

    def left_of(k):
        return jnp.where(k < nk // 2, 2, 1)

    def ready(group, k):
        left = left_of(k)
        return jnp.maximum(place_of(left, ((2 * group + c) * rows) // CHUNK), place_of(3 - left, k))

    def diag_partial(k, j):
        return pltpu.make_async_remote_copy(
            diag_part_out.at[k, j - 1], diag_part_in.at[k, j - 1], dpart_send.at[k, j - 1], dpart_recv.at[k, j - 1],
            device_id=(b, 2 * ((g + j) % ngrp) + c), device_id_type=MESH)

    def diag_final(k):
        return pltpu.make_async_remote_copy(
            diag_out.at[k], diag_in.at[k], diag_send.at[k], diag_recv.at[k],
            device_id=(jnp.where(k < nk // 2, b - 2 * e, b - e), s), device_id_type=MESH)

    def diag_multiply(t):
        def one(k, carry):
            left = left_of(k)
            for j in range(1, ngrp):
                group = (g + j) % ngrp

                @pl.when(ready(group, k) == t)
                def _():
                    diag_part_out[k, j - 1] = encode(product(left, group, 3 - left, columns(k)))
                    diag_partial(k, j).start()

            @pl.when(ready(g, k) == t)
            def _():
                diag[k] = product(left, g, 3 - left, columns(k))
            return carry

        lax.fori_loop(0, nk, one, 0)

    def diag_complete(t):
        def one(k, carry):
            @pl.when(ready(g, k) == t)
            def _():
                upper, lower = diag[k, :half, :], diag[k, half:, :]
                for j in range(1, ngrp):
                    diag_partial(k, j).wait_recv()
                    high, low = decode(diag_part_in[k, j - 1])
                    upper, lower = upper + high, lower + low
                diag_out[k] = encode(jnp.concatenate([upper, lower], axis=0))
                diag_final(k).start()
            return carry

        lax.fori_loop(0, nk, one, 0)

    for k in range(nk):
        forward_in(0, k, CHUNK).wait_recv()

    def own(k, carry):
        multiply(0, k, CHUNK, k * CHUNK)
        return carry

    lax.fori_loop(0, nk, own, 0)

    def nothing(slot, carry):
        @pl.when(jnp.logical_not(has(slot)))
        def _():
            def zeros(k, inner):
                out_ref[:, room(slot, k * CHUNK, CHUNK)] = jnp.zeros((rows, CHUNK), jnp.float32)
                return inner

            lax.fori_loop(0, nk, zeros, 0)
        return carry

    lax.fori_loop(1, 5, nothing, 0)

    def own_finish(k, carry):
        finish(0, k, CHUNK, k * CHUNK)
        return carry

    lax.fori_loop(0, nk, own_finish, 0)

    def each_slot(act):
        def one(slot, carry):
            @pl.when(has(slot))
            def _():
                act(slot)
            return carry

        lax.fori_loop(1, 4, one, 0)

    def finish_stage(p, size):
        each_slot(lambda slot: finish(slot, p, size, start_of(slot, p)))

    def stage(p, size):
        def receive(slot):
            arrival(slot, p, size).wait_recv()
            forward(slot, p, size).start()

        each_slot(receive)
        each_slot(lambda slot: forward_in(slot, p, size).wait_recv())

        @pl.when(makes)
        def _():
            diag_multiply(p)

        each_slot(lambda slot: multiply(slot, p, size, start_of(slot, p)))

    def full_stage(p, carry):
        stage(p, CHUNK)

        @pl.when(p > 0)
        def _():
            @pl.when(makes)
            def _():
                diag_complete(p - 1)
            finish_stage(p - 1, CHUNK)
        return carry

    lax.fori_loop(0, nk - 1, full_stage, 0)
    stage(nk - 1, short)

    @pl.when(makes)
    def _():
        diag_complete(nk - 2)
    finish_stage(nk - 2, CHUNK)
    stage(nk, short)

    @pl.when(makes)
    def _():
        diag_complete(nk)
    finish_stage(nk - 1, short)
    finish_stage(nk, short)

    @pl.when(has(4))
    def _():
        def one(k, carry):
            diag_final(k).wait_recv()
            high, low = decode(diag_in[k])
            keep = kept(4)
            out_ref[:half, room(4, k * CHUNK, CHUNK)] = high * keep
            out_ref[half:, room(4, k * CHUNK, CHUNK)] = low * keep
            return carry

        lax.fori_loop(0, nk, one, 0)

    def own_drain(k, carry):
        forward(0, k, CHUNK).wait_send()
        for j in range(1, ngrp):
            partial(k, j, CHUNK).wait_send()
        return carry

    lax.fori_loop(0, nk, own_drain, 0)
    for p in range(npiece):
        def drain(slot):
            forward(slot, p, sizes[p]).wait_send()
            for j in range(1, ngrp):
                partial(slot * npiece + p, j, sizes[p]).wait_send()

        each_slot(drain)

    @pl.when(makes)
    def _():
        def one(k, carry):
            for j in range(1, ngrp):
                diag_partial(k, j).wait_send()
            diag_final(k).wait_send()
            return carry

        lax.fori_loop(0, nk, one, 0)

    for j in range(1, nsamp):
        for k in range(nk):
            tell(j, k).wait_send()
    for p in range(npiece):
        for way in (1, 2, 3):
            target, copy = direct(way, p, sizes[p])

            @pl.when(inside(target))
            def _():
                copy.wait_send()


def on_device(nblk, nsamp, dosage, observed, band):
    depth, width = dosage.shape
    nk = width // CHUNK
    ngrp = nsamp // 2
    rows = width // nsamp
    npiece = nk + 1
    dma = pltpu.SemaphoreType.DMA
    coded = lambda *lead: pltpu.VMEM((*lead, rows // 2, CHUNK), jnp.int32)
    return pl.pallas_call(
        functools.partial(linkage_kernel, nblk, nsamp, nk),
        out_shape=pltpu.VMEM((rows, 5 * width), jnp.float32),
        in_specs=[
            pl.BlockSpec(memory_space=pltpu.SMEM),
            pl.BlockSpec(memory_space=pl.ANY),
            pl.BlockSpec(memory_space=pl.ANY),
        ],
        out_specs=pl.BlockSpec(memory_space=pltpu.VMEM),
        scratch_shapes=[
            pltpu.VMEM((nk, depth, CHUNK), jnp.bfloat16),
            pltpu.VMEM((nk, depth, CHUNK), jnp.int32),
            pltpu.VMEM((nsamp, nk, 8, CHUNK), jnp.float32),
            pltpu.VMEM((4, 2, width, depth), jnp.bfloat16),
            pltpu.VMEM((nk, rows, CHUNK), jnp.float32),
            coded(4 * npiece, ngrp - 1),
            coded(4 * npiece, ngrp - 1),
            coded(nk, ngrp - 1),
            coded(nk, ngrp - 1),
            coded(nk),
            coded(nk),
            dma((nk,)),
            dma((nk,)),
            dma((nsamp - 1, nk)),
            dma((nsamp - 1, nk)),
            dma((4, npiece)),
            dma((4, npiece)),
            dma((4, npiece)),
            dma((4, npiece)),
            dma((4 * npiece, ngrp - 1)),
            dma((4 * npiece, ngrp - 1)),
            dma((nk, ngrp - 1)),
            dma((nk, ngrp - 1)),
            dma((nk,)),
            dma((nk,)),
        ],
        compiler_params=pltpu.CompilerParams(
            collective_id=0, has_side_effects=True, vmem_limit_bytes=50000 * 1024
        ),
    )(band, dosage, observed)


def solution(mesh):
    return jax.shard_map(
        functools.partial(on_device, mesh.shape["snp"], mesh.shape["samp"]),
        mesh=mesh,
        in_specs=(P("samp", "snp"), P("samp", "snp"), P()),
        out_specs=P(("snp", "samp"), None),
        check_vma=False,
    )
```

profile of v0, /device:TPU:19, one launch (start us, length us, event | category | flops | bytes accessed | tf_op | source)
XLA Modules:
  0.0 89.1 jit_solution(8714693104875843374)
XLA Ops:
  0.0 0.0 copy-start
  0.0 0.7 copy-done
  0.7 86.1 %shard_map.37 = f32[256,5120]{1,0:T(8,128)S(1)} custom-call(s32[8]{0:T(128)S(1)} %copy-done, bf16[1280,1024]{1,0:T(8,128)(2,1)} %dosage_ref.1, s32[1280,1024]{1,0:T(8,128)} %observed_ref.1), custom_call_target="tpu_custom_call" | custom-call | tf_op jit(solution)/shard_map/pallas_call | solution.py:434
  86.7 2.4 %copy.5 = f32[256,5120]{1,0:T(8,128)} copy(f32[256,5120]{1,0:T(8,128)S(1)} %shard_map.37) | data formatting | bytes 10485760
Async XLA Ops:
  0.0 0.7 copy-start
where the time goes:
time: 90.2 us; the launch traced here: 89.1 us
  Pallas kernels  86.1 us (95%)
  local copies, waits for them, and re-layouts  3.02 us (3%)
    pallas_call x1, Pallas kernels, on_device(): pl.pallas_call(functools.partial(linkage_kernel, nblk, nsamp, nk), out_sh...  86.1 us
    unnamed x3, local copies, waits for them, and re-layouts  3.02 us

commit v1 on v0

--- a/solution.py
+++ b/solution.py
@@ -203,8 +203,8 @@
                     send(way, nk)
         forward(0, k, CHUNK).start()
 
-    def product(left, group, right, at):
-        own_rows = pl.ds(pl.multiple_of((2 * group + c) * rows, rows), rows)
+    def product(left, group, right, at, low=0, size=rows):
+        own_rows = pl.ds(pl.multiple_of((2 * group + c) * rows + low, size), size)
         both = [
             lax.dot_general(
                 zt[left, h, own_rows, :], zt[right, h, at, :], (((1,), (1,)), ((), ())),
@@ -245,55 +245,80 @@
 
     makes = has(1) & has(2)
 
+    quarter = half // 2
+
     def left_of(k):
         return jnp.where(k < nk // 2, 2, 1)
 
-    def ready(group, k):
+    def ready(group, u):
+        k = u // 2
         left = left_of(k)
-        return jnp.maximum(place_of(left, ((2 * group + c) * rows) // CHUNK), place_of(3 - left, k))
-
-    def diag_partial(k, j):
-        return pltpu.make_async_remote_copy(
-            diag_part_out.at[k, j - 1], diag_part_in.at[k, j - 1], dpart_send.at[k, j - 1], dpart_recv.at[k, j - 1],
+        first_row = (2 * group + c) * rows + (u % 2) * half
+        place = place_of(left, first_row // CHUNK)
+        place = jnp.where(place == nk, nk - 1 + (first_row % CHUNK) // short, place)
+        return jnp.maximum(place, place_of(3 - left, k))
+
+    def diag_partial(u, j):
+        return pltpu.make_async_remote_copy(
+            diag_part_out.at[u, j - 1], diag_part_in.at[u, j - 1], dpart_send.at[u, j - 1], dpart_recv.at[u, j - 1],
             device_id=(b, 2 * ((g + j) % ngrp) + c), device_id_type=MESH)
 
-    def diag_final(k):
-        return pltpu.make_async_remote_copy(
-            diag_out.at[k], diag_in.at[k], diag_send.at[k], diag_recv.at[k],
-            device_id=(jnp.where(k < nk // 2, b - 2 * e, b - e), s), device_id_type=MESH)
-
-    def diag_multiply(t):
-        def one(k, carry):
-            left = left_of(k)
+    def diag_final(u):
+        return pltpu.make_async_remote_copy(
+            diag_out.at[u], diag_in.at[u], diag_send.at[u], diag_recv.at[u],
+            device_id=(jnp.where(u < nk, b - 2 * e, b - e), s), device_id_type=MESH)
+
+    def diag_product(group, u):
+        left = left_of(u // 2)
+        return product(left, group, 3 - left, columns(u // 2), (u % 2) * half, half)
+
+    def each_unit(group, p, act):
+        def one(u, carry):
+            @pl.when(ready(group, u) == p)
+            def _():
+                act(u)
+            return carry
+
+        lax.fori_loop(0, 2 * nk, one, 0)
+
+    def diag_multiply(p):
+        for j in range(1, ngrp):
+            group = (g + j) % ngrp
+
+            def away(u):
+                diag_part_out[u, j - 1] = encode(diag_product(group, u))
+                diag_partial(u, j).start()
+
+            each_unit(group, p, away)
+
+        def here(u):
+            diag[u] = diag_product(g, u)
+
+        each_unit(g, p, here)
+
+    def diag_complete(p):
+        def act(u):
+            upper, lower = diag[u, :quarter, :], diag[u, quarter:, :]
             for j in range(1, ngrp):
-                group = (g + j) % ngrp
-
-                @pl.when(ready(group, k) == t)
-                def _():
-                    diag_part_out[k, j - 1] = encode(product(left, group, 3 - left, columns(k)))
-                    diag_partial(k, j).start()
-
-            @pl.when(ready(g, k) == t)
-            def _():
-                diag[k] = product(left, g, 3 - left, columns(k))
-            return carry
-
-        lax.fori_loop(0, nk, one, 0)
-
-    def diag_complete(t):
-        def one(k, carry):
-            @pl.when(ready(g, k) == t)
-            def _():
-                upper, lower = diag[k, :half, :], diag[k, half:, :]
-                for j in range(1, ngrp):
-                    diag_partial(k, j).wait_recv()
-                    high, low = decode(diag_part_in[k, j - 1])
-                    upper, lower = upper + high, lower + low
-                diag_out[k] = encode(jnp.concatenate([upper, lower], axis=0))
-                diag_final(k).start()
-            return carry
-
-        lax.fori_loop(0, nk, one, 0)
+                diag_partial(u, j).wait_recv()
+                high, low = decode(diag_part_in[u, j - 1])
+                upper, lower = upper + high, lower + low
+            diag_out[u] = encode(jnp.concatenate([upper, lower], axis=0))
+            diag_final(u).start()
+
+        each_unit(g, p, act)
+
+    def diag_receive(p):
+        def act(u):
+            diag_final(u).wait_recv()
+            high, low = decode(diag_in[u])
+            keep = kept(4)
+            to = room(4, (u // 2) * CHUNK, CHUNK)
+            row = (u % 2) * half
+            out_ref[pl.ds(pl.multiple_of(row, quarter), quarter), to] = high * keep
+            out_ref[pl.ds(pl.multiple_of(row + quarter, quarter), quarter), to] = low * keep
+
+        each_unit(g, p, act)
 
     for k in range(nk):
         forward_in(0, k, CHUNK).wait_recv()
@@ -339,14 +364,40 @@
             arrival(slot, p, size).wait_recv()
             forward(slot, p, size).start()
 
-        each_slot(receive)
-        each_slot(lambda slot: forward_in(slot, p, size).wait_recv())
+        @pl.when(has(2))
+        def _():
+            receive(2)
+            forward_in(2, p, size).wait_recv()
+            multiply(2, p, size, start_of(2, p))
+
+        def others(act):
+            def one(n, carry):
+                slot = 1 + 2 * n
+
+                @pl.when(has(slot))
+                def _():
+                    act(slot)
+                return carry
+
+            lax.fori_loop(0, 2, one, 0)
+
+        others(receive)
+
+        @pl.when(has(1))
+        def _():
+            forward_in(1, p, size).wait_recv()
 
         @pl.when(makes)
         def _():
             diag_multiply(p)
 
-        each_slot(lambda slot: multiply(slot, p, size, start_of(slot, p)))
+        def rest(slot):
+            @pl.when(slot == 3)
+            def _():
+                forward_in(3, p, size).wait_recv()
+            multiply(slot, p, size, start_of(slot, p))
+
+        others(rest)
 
     def full_stage(p, carry):
         stage(p, CHUNK)
@@ -366,25 +417,34 @@
     def _():
         diag_complete(nk - 2)
     finish_stage(nk - 2, CHUNK)
+
+    def early(p, carry):
+        diag_receive(p)
+        return carry
+
+    @pl.when(has(4))
+    def _():
+        lax.fori_loop(0, nk - 2, early, 0)
     stage(nk, short)
 
     @pl.when(makes)
     def _():
+        diag_complete(nk - 1)
+    finish_stage(nk - 1, short)
+
+    @pl.when(makes)
+    def _():
         diag_complete(nk)
-    finish_stage(nk - 1, short)
+
+    @pl.when(has(4))
+    def _():
+        diag_receive(nk - 2)
     finish_stage(nk, short)
 
     @pl.when(has(4))
     def _():
-        def one(k, carry):
-            diag_final(k).wait_recv()
-            high, low = decode(diag_in[k])
-            keep = kept(4)
-            out_ref[:half, room(4, k * CHUNK, CHUNK)] = high * keep
-            out_ref[half:, room(4, k * CHUNK, CHUNK)] = low * keep
-            return carry
-
-        lax.fori_loop(0, nk, one, 0)
+        diag_receive(nk - 1)
+        diag_receive(nk)
 
     def own_drain(k, carry):
         forward(0, k, CHUNK).wait_send()
@@ -403,13 +463,13 @@
 
     @pl.when(makes)
     def _():
-        def one(k, carry):
+        def one(u, carry):
             for j in range(1, ngrp):
-                diag_partial(k, j).wait_send()
-            diag_final(k).wait_send()
+                diag_partial(u, j).wait_send()
+            diag_final(u).wait_send()
             return carry
 
-        lax.fori_loop(0, nk, one, 0)
+        lax.fori_loop(0, 2 * nk, one, 0)
 
     for j in range(1, nsamp):
         for k in range(nk):
@@ -430,7 +490,7 @@
     rows = width // nsamp
     npiece = nk + 1
     dma = pltpu.SemaphoreType.DMA
-    coded = lambda *lead: pltpu.VMEM((*lead, rows // 2, CHUNK), jnp.int32)
+    coded = lambda *lead: pltpu.VMEM((*lead, CHUNK), jnp.int32)
     return pl.pallas_call(
         functools.partial(linkage_kernel, nblk, nsamp, nk),
         out_shape=pltpu.VMEM((rows, 5 * width), jnp.float32),
@@ -445,13 +505,13 @@
             pltpu.VMEM((nk, depth, CHUNK), jnp.int32),
             pltpu.VMEM((nsamp, nk, 8, CHUNK), jnp.float32),
             pltpu.VMEM((4, 2, width, depth), jnp.bfloat16),
-            pltpu.VMEM((nk, rows, CHUNK), jnp.float32),
-            coded(4 * npiece, ngrp - 1),
-            coded(4 * npiece, ngrp - 1),
-            coded(nk, ngrp - 1),
-            coded(nk, ngrp - 1),
-            coded(nk),
-            coded(nk),
+            pltpu.VMEM((2 * nk, rows // 2, CHUNK), jnp.float32),
+            coded(4 * npiece, ngrp - 1, rows // 2),
+            coded(4 * npiece, ngrp - 1, rows // 2),
+            coded(2 * nk, ngrp - 1, rows // 4),
+            coded(2 * nk, ngrp - 1, rows // 4),
+            coded(2 * nk, rows // 4),
+            coded(2 * nk, rows // 4),
             dma((nk,)),
             dma((nk,)),
             dma((nsamp - 1, nk)),
@@ -462,13 +522,13 @@
             dma((4, npiece)),
             dma((4 * npiece, ngrp - 1)),
             dma((4 * npiece, ngrp - 1)),
-            dma((nk, ngrp - 1)),
-            dma((nk, ngrp - 1)),
-            dma((nk,)),
-            dma((nk,)),
+            dma((2 * nk, ngrp - 1)),
+            dma((2 * nk, ngrp - 1)),
+            dma((2 * nk,)),
+            dma((2 * nk,)),
         ],
         compiler_params=pltpu.CompilerParams(
-            collective_id=0, has_side_effects=True, vmem_limit_bytes=50000 * 1024
+            collective_id=0, has_side_effects=True, vmem_limit_bytes=59000 * 1024
         ),
     )(band, dosage, observed)
 

time: 90.2 us -> 96.1 us (1.065)
  Pallas kernels: 86.1 us -> 92.4 us
    pallas_call x1, Pallas kernels: 86.1 us -> 92.4 us  [on_device(): pl.pallas_call(functools.partial(linkage_kernel, nblk, nsamp, nk), out_sh...]
    unnamed x3 -> x1, local copies, waits for them, and re-layouts: 3.02 us -> 2.36 us
where the time goes in v1:
time: 96.1 us; the launch traced here: 94.8 us
  Pallas kernels  92.4 us (96%)
  local copies, waits for them, and re-layouts  2.36 us (2%)
    pallas_call x1, Pallas kernels, on_device(): pl.pallas_call(functools.partial(linkage_kernel, nblk, nsamp, nk), out_sh...  92.4 us
    unnamed x1, local copies, waits for them, and re-layouts  2.36 us

profile of v1, /device:TPU:19, one launch (start us, length us, event | category | flops | bytes accessed | tf_op | source)
XLA Modules:
  0.0 94.8 jit_solution(16756169338408753312)
XLA Ops:
  0.0 92.4 %shard_map.37 = f32[256,5120]{1,0:T(8,128)S(1)} custom-call(s32[8]{0:T(128)} %band_ref.1, bf16[1280,1024]{1,0:T(8,128)(2,1)} %dosage_ref.1, s32[1280,1024]{1,0:T(8,128)} %observed_ref.1), custom_call_target="tpu_custom_call" | custom-call | tf_op jit(solution)/shard_map/pallas_call | solution.py:494
  92.5 2.4 %copy.5 = f32[256,5120]{1,0:T(8,128)} copy(f32[256,5120]{1,0:T(8,128)S(1)} %shard_map.37) | data formatting | bytes 10485760

commit v2 on v1

--- a/solution.py
+++ b/solution.py
@@ -112,7 +112,7 @@
             stats.at[other, k], stats.at[other, k], stat_send.at[j - 1, k], stat_recv.at[j - 1, k],
             device_id=(b, other), device_id_type=MESH)
 
-    for k in range(nk):
+    def gather(k):
         for copy in load(k):
             copy.wait()
 
@@ -169,7 +169,7 @@
         def _():
             copy.start()
 
-    for k in range(nk):
+    def spread(k):
         for j in range(1, nsamp):
             hear(j, k).wait_recv()
         part = stats[0, k]
@@ -203,8 +203,14 @@
                     send(way, nk)
         forward(0, k, CHUNK).start()
 
-    def product(left, group, right, at, low=0, size=rows):
-        own_rows = pl.ds(pl.multiple_of((2 * group + c) * rows + low, size), size)
+    gather(0)
+    for k in range(nk):
+        if k + 1 < nk:
+            gather(k + 1)
+        spread(k)
+
+    def product(left, group, right, at):
+        own_rows = pl.ds(pl.multiple_of((2 * group + c) * rows, rows), rows)
         both = [
             lax.dot_general(
                 zt[left, h, own_rows, :], zt[right, h, at, :], (((1,), (1,)), ((), ())),
@@ -218,13 +224,20 @@
             part_out.at[i, j - 1, :, 0:size], part_in.at[i, j - 1, :, 0:size], part_send.at[i, j - 1], part_recv.at[i, j - 1],
             device_id=(b, 2 * ((g + j) % ngrp) + c), device_id_type=MESH)
 
-    def multiply(slot, p, size, start):
+    def multiply_away(slot, p, size, start):
         i = slot * npiece + p
         at = pl.ds(pl.multiple_of(start, short), size)
         for j in range(1, ngrp):
             part_out[i, j - 1, :, 0:size] = encode(product(0, (g + j) % ngrp, slot, at))
             partial(i, j, size).start()
+
+    def multiply_here(slot, size, start):
+        at = pl.ds(pl.multiple_of(start, short), size)
         out_ref[:, room(slot, start, size)] = product(0, g, slot, at)
+
+    def multiply(slot, p, size, start):
+        multiply_away(slot, p, size, start)
+        multiply_here(slot, size, start)
 
     def kept(slot):
         offset = offset_of(slot, e)
@@ -245,18 +258,14 @@
 
     makes = has(1) & has(2)
 
-    quarter = half // 2
-
-    def left_of(k):
-        return jnp.where(k < nk // 2, 2, 1)
-
-    def ready(group, u):
-        k = u // 2
-        left = left_of(k)
-        first_row = (2 * group + c) * rows + (u % 2) * half
-        place = place_of(left, first_row // CHUNK)
-        place = jnp.where(place == nk, nk - 1 + (first_row % CHUNK) // short, place)
-        return jnp.maximum(place, place_of(3 - left, k))
+
+    def left_of(group, k):
+        j = ((2 * group + c) * rows) // CHUNK
+        return jnp.where(jnp.where((j == 0) | (j == nk - 1), k != nk - 1, k == 1), 2, 1)
+
+    def ready(group, k):
+        left = left_of(group, k)
+        return jnp.maximum(place_of(left, ((2 * group + c) * rows) // CHUNK), place_of(3 - left, k))
 
     def diag_partial(u, j):
         return pltpu.make_async_remote_copy(
@@ -266,11 +275,11 @@
     def diag_final(u):
         return pltpu.make_async_remote_copy(
             diag_out.at[u], diag_in.at[u], diag_send.at[u], diag_recv.at[u],
-            device_id=(jnp.where(u < nk, b - 2 * e, b - e), s), device_id_type=MESH)
+            device_id=(b - e * left_of(g, u), s), device_id_type=MESH)
 
     def diag_product(group, u):
-        left = left_of(u // 2)
-        return product(left, group, 3 - left, columns(u // 2), (u % 2) * half, half)
+        left = left_of(group, u)
+        return product(left, group, 3 - left, columns(u))
 
     def each_unit(group, p, act):
         def one(u, carry):
@@ -279,9 +288,9 @@
                 act(u)
             return carry
 
-        lax.fori_loop(0, 2 * nk, one, 0)
-
-    def diag_multiply(p):
+        lax.fori_loop(0, nk, one, 0)
+
+    def diag_away(p):
         for j in range(1, ngrp):
             group = (g + j) % ngrp
 
@@ -291,6 +300,7 @@
 
             each_unit(group, p, away)
 
+    def diag_here(p):
         def here(u):
             diag[u] = diag_product(g, u)
 
@@ -298,25 +308,33 @@
 
     def diag_complete(p):
         def act(u):
-            upper, lower = diag[u, :quarter, :], diag[u, quarter:, :]
+            upper, lower = diag[u, :half, :], diag[u, half:, :]
             for j in range(1, ngrp):
                 diag_partial(u, j).wait_recv()
                 high, low = decode(diag_part_in[u, j - 1])
                 upper, lower = upper + high, lower + low
             diag_out[u] = encode(jnp.concatenate([upper, lower], axis=0))
-            diag_final(u).start()
 
         each_unit(g, p, act)
+
+    def deliver(p):
+        each_unit(g, p, lambda u: diag_final(u).start())
+
+    def each_place(act):
+        def one(p, carry):
+            act(p)
+            return carry
+
+        lax.fori_loop(0, nk - 1, one, 0)
 
     def diag_receive(p):
         def act(u):
             diag_final(u).wait_recv()
             high, low = decode(diag_in[u])
             keep = kept(4)
-            to = room(4, (u // 2) * CHUNK, CHUNK)
-            row = (u % 2) * half
-            out_ref[pl.ds(pl.multiple_of(row, quarter), quarter), to] = high * keep
-            out_ref[pl.ds(pl.multiple_of(row + quarter, quarter), quarter), to] = low * keep
+            to = room(4, u * CHUNK, CHUNK)
+            out_ref[:half, to] = high * keep
+            out_ref[half:, to] = low * keep
 
         each_unit(g, p, act)
 
@@ -359,45 +377,26 @@
     def finish_stage(p, size):
         each_slot(lambda slot: finish(slot, p, size, start_of(slot, p)))
 
-    def stage(p, size):
+    def stage(p, size, last=False):
         def receive(slot):
             arrival(slot, p, size).wait_recv()
             forward(slot, p, size).start()
 
-        @pl.when(has(2))
-        def _():
-            receive(2)
-            forward_in(2, p, size).wait_recv()
-            multiply(2, p, size, start_of(2, p))
-
-        def others(act):
-            def one(n, carry):
-                slot = 1 + 2 * n
-
-                @pl.when(has(slot))
-                def _():
-                    act(slot)
-                return carry
-
-            lax.fori_loop(0, 2, one, 0)
-
-        others(receive)
-
-        @pl.when(has(1))
-        def _():
-            forward_in(1, p, size).wait_recv()
+        each_slot(receive)
+        each_slot(lambda slot: forward_in(slot, p, size).wait_recv())
 
         @pl.when(makes)
         def _():
-            diag_multiply(p)
-
-        def rest(slot):
-            @pl.when(slot == 3)
-            def _():
-                forward_in(3, p, size).wait_recv()
-            multiply(slot, p, size, start_of(slot, p))
-
-        others(rest)
+            if last:
+                each_place(deliver)
+            diag_away(p)
+            diag_here(p)
+
+        if last:
+            each_slot(lambda slot: multiply_away(slot, p, size, start_of(slot, p)))
+            each_slot(lambda slot: multiply_here(slot, size, start_of(slot, p)))
+        else:
+            each_slot(lambda slot: multiply(slot, p, size, start_of(slot, p)))
 
     def full_stage(p, carry):
         stage(p, CHUNK)
@@ -418,32 +417,18 @@
         diag_complete(nk - 2)
     finish_stage(nk - 2, CHUNK)
 
-    def early(p, carry):
-        diag_receive(p)
-        return carry
-
-    @pl.when(has(4))
-    def _():
-        lax.fori_loop(0, nk - 2, early, 0)
-    stage(nk, short)
-
-    @pl.when(makes)
-    def _():
-        diag_complete(nk - 1)
-    finish_stage(nk - 1, short)
+    stage(nk, short, last=True)
 
     @pl.when(makes)
     def _():
         diag_complete(nk)
+        deliver(nk)
+    finish_stage(nk - 1, short)
+    finish_stage(nk, short)
 
     @pl.when(has(4))
     def _():
-        diag_receive(nk - 2)
-    finish_stage(nk, short)
-
-    @pl.when(has(4))
-    def _():
-        diag_receive(nk - 1)
+        each_place(diag_receive)
         diag_receive(nk)
 
     def own_drain(k, carry):
@@ -469,7 +454,7 @@
             diag_final(u).wait_send()
             return carry
 
-        lax.fori_loop(0, 2 * nk, one, 0)
+        lax.fori_loop(0, nk, one, 0)
 
     for j in range(1, nsamp):
         for k in range(nk):
@@ -505,13 +490,13 @@
             pltpu.VMEM((nk, depth, CHUNK), jnp.int32),
             pltpu.VMEM((nsamp, nk, 8, CHUNK), jnp.float32),
             pltpu.VMEM((4, 2, width, depth), jnp.bfloat16),
-            pltpu.VMEM((2 * nk, rows // 2, CHUNK), jnp.float32),
+            pltpu.VMEM((nk, rows, CHUNK), jnp.float32),
             coded(4 * npiece, ngrp - 1, rows // 2),
             coded(4 * npiece, ngrp - 1, rows // 2),
-            coded(2 * nk, ngrp - 1, rows // 4),
-            coded(2 * nk, ngrp - 1, rows // 4),
-            coded(2 * nk, rows // 4),
-            coded(2 * nk, rows // 4),
+            coded(nk, ngrp - 1, rows // 2),
+            coded(nk, ngrp - 1, rows // 2),
+            coded(nk, rows // 2),
+            coded(nk, rows // 2),
             dma((nk,)),
             dma((nk,)),
             dma((nsamp - 1, nk)),
@@ -522,10 +507,10 @@
             dma((4, npiece)),
             dma((4 * npiece, ngrp - 1)),
             dma((4 * npiece, ngrp - 1)),
-            dma((2 * nk, ngrp - 1)),
-            dma((2 * nk, ngrp - 1)),
-            dma((2 * nk,)),
-            dma((2 * nk,)),
+            dma((nk, ngrp - 1)),
+            dma((nk, ngrp - 1)),
+            dma((nk,)),
+            dma((nk,)),
         ],
         compiler_params=pltpu.CompilerParams(
             collective_id=0, has_side_effects=True, vmem_limit_bytes=59000 * 1024

time: 96.1 us -> 89 us (0.926); the launches traced: 94.8 us -> 88.7 us
  Pallas kernels: 92.4 us -> 86.3 us
    pallas_call x1, Pallas kernels: 92.4 us -> 86.3 us  [on_device(): pl.pallas_call(functools.partial(linkage_kernel, nblk, nsamp, nk), out_sh...]
where the time goes in v2:
time: 89 us; the launch traced here: 88.7 us
  Pallas kernels  86.3 us (97%)
  local copies, waits for them, and re-layouts  2.36 us (3%)
    pallas_call x1, Pallas kernels, on_device(): pl.pallas_call(functools.partial(linkage_kernel, nblk, nsamp, nk), out_sh...  86.3 us
    unnamed x1, local copies, waits for them, and re-layouts  2.36 us

profile of v2, /device:TPU:19, one launch (start us, length us, event | category | flops | bytes accessed | tf_op | source)
XLA Modules:
  0.0 88.7 jit_solution(18355930432997111973)
XLA Ops:
  0.0 86.3 %shard_map.37 = f32[256,5120]{1,0:T(8,128)S(1)} custom-call(s32[8]{0:T(128)} %band_ref.1, bf16[1280,1024]{1,0:T(8,128)(2,1)} %dosage_ref.1, s32[1280,1024]{1,0:T(8,128)} %observed_ref.1), custom_call_target="tpu_custom_call" | custom-call | tf_op jit(solution)/shard_map/pallas_call | solution.py:479
  86.3 2.4 %copy.5 = f32[256,5120]{1,0:T(8,128)} copy(f32[256,5120]{1,0:T(8,128)S(1)} %shard_map.37) | data formatting | bytes 10485760
